TPU v7x, 256 devices: a whole 4x4x8 slice. The times are simulated.
256 devices in a mesh: band: 4 (over x), grid: 64 (over z, y, core).
Axes of the slice: x: 4, y: 4, z: 8, core: 2. Of those that a mesh axis runs over, the one named last changes fastest.
Arguments:
- orbitals: float32 [256, 512, 1024], P('band', 'grid'), may hold values from -6 to 6
- potentials: bfloat16 [2048, 512, 1024], P(None, 'grid', 'band'), may hold values from -0.0078125 to 0.0078125
- point_rows: int32 [2048], replicated, may hold values from 0 to 511
- point_cols: int32 [2048], replicated, may hold values from 0 to 1023
Outputs:
- exchanged: float32 [256, 512, 1024], P('band', 'grid')
All inputs are finite; a program needn't handle non-finite values.
Results may differ from a plain program's by a relative error of at most 0.0003.
Values sent between devices are 32-bit elements; how exact they have to be, the bound alone decides.
A program may use at most 128 MiB of HBM per device.

v0:
```python
import jax
import jax.numpy as jnp
from jax import lax
from jax.sharding import PartitionSpec as P


def local(orbitals, potentials, point_rows, point_cols):
    rows_here = orbitals.shape[1]
    start_row = lax.axis_index("grid") * rows_here
    local_rows = point_rows - start_row
    row_inside = (local_rows >= 0) & (local_rows < rows_here)
    safe_rows = jnp.clip(local_rows, 0, rows_here - 1)
    owned_block = lax.all_to_all(orbitals, "band", split_axis=2, concat_axis=0, tiled=True)
    cols_here = owned_block.shape[2]
    local_cols = point_cols - lax.axis_index("band") * cols_here
    inside = row_inside & (local_cols >= 0) & (local_cols < cols_here)
    picked = owned_block[:, safe_rows, jnp.clip(local_cols, 0, cols_here - 1)]
    partial_value = jnp.where(inside[None, :], picked, jnp.zeros_like(picked))
    point_panel = lax.psum(partial_value, ("band", "grid"))
    bands_all, rows_own, cols_own = owned_block.shape
    cells = rows_own * cols_own
    flat_block = owned_block.reshape(bands_all, cells)
    kernel = jnp.dot(
        point_panel.T,
        flat_block,
        precision=lax.Precision.HIGHEST,
        preferred_element_type=jnp.float32,
    )
    weighted = kernel * potentials.reshape(potentials.shape[0], cells).astype(jnp.float32)
    result = -jnp.dot(
        point_panel, weighted, precision=lax.Precision.HIGHEST, preferred_element_type=jnp.float32
    )
    result = result.reshape(bands_all, rows_own, cols_own)
    return lax.all_to_all(result, "band", split_axis=0, concat_axis=2, tiled=True)


def solution(mesh):
    in_specs = (P("band", "grid", None), P(None, "grid", "band"), P(), P())
    out_specs = P("band", "grid", None)
    return jax.shard_map(local, mesh=mesh, in_specs=in_specs, out_specs=out_specs, check_vma=False)
```

profile of v0, /device:TPU:8, one launch (start us, length us, event | category | flops | bytes accessed | tf_op | source)
XLA Modules:
  0.0 435.3 jit_solution(5763142422010801127)
XLA Ops:
  6.5 4.3 copy.19
  10.9 5.5 %reshape.32 = f32[4,1,131072]{2,1,0:T(1,128)} reshape(f32[1024,8,64]{2,1,0:T(8,128)} %bitcast.26) | data formatting | bytes 4194304
  16.4 0.0 copy-start.3
  16.4 0.0 copy-start.4
  16.4 4.4 %all-to-all-start = ((f32[4,1,131072]{2,1,0:T(1,128)}), f32[4,1,131072]{2,1,0:T(1,128)S(1)}, u32[]{:S(2)}, u32[]{:S(2)}) async-start(f32[4,1,131072]{2,1,0:T(1,128)} %reshape.32), calls=%async_computation | async-start | bytes 4194304 | tf_op jit(solution)/shard_map/all_to_all | solution.py:13
  20.8 0.0 all-reduce.2.cloned.1.call-start
  20.8 0.0 copy-done.3
  20.8 0.0 copy-done.4
  20.8 26.3 %all-to-all-done = f32[4,1,131072]{2,1,0:T(1,128)S(1)} async-done(((f32[4,1,131072]{2,1,0:T(1,128)}), f32[4,1,131072]{2,1,0:T(1,128)S(1)}, u32[]{:S(2)}, u32[]{:S(2)}) %all-to-all-start) | async-done | bytes 2097184 | tf_op jit(solution)/shard_map/all_to_all | solution.py:13
  47.1 0.0 copy-start.2
  47.1 1.3 copy-done.2
  48.4 0.5 broadcast.49
  49.0 7.7 %reduce = f32[4,131072]{1,0:T(4,128)S(1)} reduce(f32[4,1,131072]{2,1,0:T(1,128)} %copy-done.2, f32[]{:T(128)} %broadcast.49), dimensions={1}, to_apply=%all_to_all.26.reduce_sub_computation | reduce | bytes 4194308 | tf_op jit(solution)/shard_map/all_to_all | solution.py:13
  56.7 3.9 reshape.33
  60.6 3.9 copy.25
  64.5 1.7 copy.21
  66.2 1.9 copy.22
  68.1 23.8 %gather_fusion = f32[2048,256]{1,0:T(8,128)} fusion(f32[256,8,256]{0,2,1:T(8,128)S(1)} %copy.22, s32[2048]{0:T(1024)S(1)} %fusion.7), kind=kCustom, calls=%fused_computation | custom fusion | bytes 4210688 | tf_op jit(solution)/shard_map/gather | solution.py:17
  92.0 3.3 select_bitcast_fusion
  95.2 0.0 all-reduce.2.cloned.1.call-update
  95.2 0.0 copy-start
  95.3 13.5 %copy.27 = f32[256,8,8,256]{3,1,2,0:T(8,128)} copy(bf16[256,8,8,256]{3,2,1,0:T(8,128)(2,1)} %bitcast.27) | data formatting | bytes 25165824
  108.8 0.0 copy-done
  108.8 0.9 copy.26
  109.6 250.4 %all-reduce.2.cloned.1.call-done = f32[256,2048]{0,1:T(8,128)} async-done(((f32[256,2048]{0,1:T(8,128)}), f32[256,2048]{0,1:T(8,128)}) %all-reduce.2.cloned.1.call-update) | async-done | bytes 2097168 | tf_op jit(solution)/shard_map/psum | solution.py:19
  360.0 0.0 copy-start.1
  360.0 17.3 %fusion.10 = f32[2048,2048]{1,0:T(8,128)} fusion(f32[256,2048]{0,1:T(8,128)} %all-reduce.2.cloned.1.call-done, f32[256,2048]{1,0:T(8,128)S(1)} %bitcast.28), kind=kOutput, calls=%fused_computation.13 | convolution fusion | flops 12884901888 | bytes 20971520 | tf_op jit(solution)/shard_map/dot_general | solution.py:23
  377.3 0.0 copy-done.1
  377.3 19.9 %fusion.2 = f32[256,2048]{1,0:T(8,128)S(1)} fusion(f32[256,2048]{0,1:T(8,128)S(1)} %copy-done.1, f32[2048,2048]{1,0:T(8,128)} %fusion.10, f32[2048,2048]{1,0:T(8,128)} %bitcast.22), kind=kOutput, calls=%fused_computation.3 | convolution fusion | flops 12889620480 | bytes 37748736 | tf_op jit(solution)/shard_map/dot_general | solution.py:30
  397.2 0.9 copy.28
  398.1 28.8 %all_to_all.36 = f32[256,8,256]{2,1,0:T(8,128)S(1)} all-to-all(f32[256,8,256]{2,1,0:T(8,128)S(1)} %bitcast.31), channel_id=1, replica_groups=mesh['band'=4,'grid'=64] {'band'}, dimensions={0} | all-to-all | bytes 4194304 | tf_op jit(solution)/shard_map/all_to_all | solution.py:34
  426.9 1.6 copy.24
  (2 shorter events, 0.0 us)
Async XLA Ops:
  16.4 4.4 %copy-start.3 = (s32[2048]{0:T(1024)S(1)}, s32[2048]{0:T(1024)}, u32[]{:S(2)}) copy-start(s32[2048]{0:T(1024)} %param.7) | copy-start | bytes 24580
  16.4 4.4 %copy-start.4 = (s32[2048]{0:T(1024)S(1)}, s32[2048]{0:T(1024)}, u32[]{:S(2)}) copy-start(s32[2048]{0:T(1024)} %param.6) | copy-start | bytes 24580
  16.4 30.8 %all-to-all-start = ((f32[4,1,131072]{2,1,0:T(1,128)}), f32[4,1,131072]{2,1,0:T(1,128)S(1)}, u32[]{:S(2)}, u32[]{:S(2)}) async-start(f32[4,1,131072]{2,1,0:T(1,128)} %reshape.32), calls=%async_computation | async-start | bytes 4194304 | tf_op jit(solution)/shard_map/all_to_all | solution.py:13
  20.8 339.2 %all-reduce.2.cloned.1.call-start = ((), (), s32[]{:S(2)}) async-start(), calls=%async_computation.2 | async-start | bytes 4194304 | tf_op jit(solution)/shard_map/psum | solution.py:19
  47.1 1.3 copy-start.2
  95.2 13.5 %copy-start = (f32[4,64,8,256]{3,2,1,0:T(8,128)S(1)}, f32[4,64,8,256]{3,2,1,0:T(8,128)}, u32[]{:S(2)}) copy-start(f32[4,64,8,256]{3,2,1,0:T(8,128)} %copy.21) | copy-start | bytes 6291460
  360.0 17.3 %copy-start.1 = (f32[256,2048]{0,1:T(8,128)S(1)}, f32[256,2048]{0,1:T(8,128)}, u32[]{:S(2)}) copy-start(f32[256,2048]{0,1:T(8,128)} %all-reduce.2.cloned.1.call-done) | copy-start | bytes 6291460
Sparse Core Ops, SparseCore 0:
  95.4 264.6 all-reduce.1
where the time goes:
time: 436 us; the launch traced here: 435 us
  waiting for transfers between devices  277 us (64%)
  local copies, waits for them, and re-layouts  63.8 us (15%)
  matrix products  37.2 us (9%)
  blocking collectives  28.8 us (7%)
  between operations  13.5 us (3%)
  other arithmetic  11 us (3%)
  starting transfers between devices  4.43 us (1%)
    psum x1, waiting for transfers between devices, local(): point_panel = lax.psum(partial_value, ('band', 'grid'))  250 us
    unnamed x16, local copies, waits for them, and re-layouts  30.4 us
    all_to_all x1, blocking collectives, local(): lax.all_to_all(result, 'band', split_axis=0, concat_axis=2, tiled=True)  28.8 us
    all_to_all x1, waiting for transfers between devices, local(): lax.all_to_all(orbitals, 'band', split_axis=2, concat_axis=0, tiled=True)  26.3 us
    gather x1, local copies, waits for them, and re-layouts, local(): picked = owned_block[:, safe_rows, jnp.clip(local_cols, 0, cols_here - 1)]  23.8 us
    dot_general x1, matrix products, local(): jnp.dot(point_panel, weighted, precision=lax.Precision.HIGHEST, preferred...  19.9 us
    dot_general x1, matrix products, local(): jnp.dot(point_panel.T, flat_block, precision=lax.Precision.HIGHEST, prefe...  17.3 us
  transfers between devices with their start and end apart: 2, of which 2 were waited for; matrix products, arithmetic and copies ran while one was open for 3% of the time, Pallas kernels for 0%

commit v1 on v0

v1 whole, which is shorter than its diff:
```python
import jax
import jax.numpy as jnp
from jax import lax
from jax.experimental import pallas as pl
from jax.experimental.pallas import tpu as pltpu
from jax.sharding import PartitionSpec as P

MESH = pl.DeviceIdType.MESH
BF = jnp.bfloat16
F32 = jnp.float32
MC = 512


def split(v):
    hi = v.astype(BF)
    return hi, (v - hi.astype(F32)).astype(BF)


def body(orb, pot, rows, cols, y_out,
         orbv, vraw, vrow, amat, orecv, ohi, olo, qa, ra, qb, rb, qc, rc, qd, rd,
         pt, pth, ptl, ph, plo, ysend,
         lsem, in_s, in_r, a_s, a_r, b_s, b_r, c_s, c_r, d_s, d_r,
         z_s, z_r, y_s, y_r, k_s, k_r, o_s, o_r, o_l):
    x = lax.axis_index("band")
    g = lax.axis_index("grid")
    z, y, c = g // 8, (g // 2) % 4, g % 2

    def dev(xx, zz, yy, cc):
        return (xx, (zz * 4 + yy) * 2 + cc)

    def xpeer(d):
        return dev((x + d) % 4, z, y, c)

    def zpeer(d):
        return dev(x, (z + d) % 8, y, c)

    def ypeer(d):
        return dev(x, z, (y + d) % 4, c)

    partner = dev(x, z, y, 1 - c)

    def remote(src, dst, ss, rs, to):
        return pltpu.make_async_remote_copy(
            src_ref=src, dst_ref=dst, send_sem=ss, recv_sem=rs,
            device_id=to, device_id_type=MESH)

    load_orb = [pltpu.make_async_copy(orb.at[:, pl.ds(128 * t, 128)], orbv.at[t], lsem.at[t])
                for t in range(8)]
    for cp in load_orb:
        cp.start()
    load_pot = pltpu.make_async_copy(pot, vraw, lsem.at[10])
    load_pot.start()

    def columns(to, t):
        return orb.at[:, pl.ds(pl.multiple_of(256 * to + 128 * t, 128), 128)]

    def landing(t):
        return orecv.at[t, pl.ds(pl.multiple_of(512 * x, 512), 512), :]

    load_own = [pltpu.make_async_copy(columns(x, t), landing(t), lsem.at[8 + t]) for t in range(2)]
    for cp in load_own:
        cp.start()

    barrier = pltpu.get_barrier_semaphore()
    peers = ([partner] + [xpeer(d) for d in (1, 2, 3)] + [ypeer(d) for d in (1, 2, 3)]
             + [zpeer(d) for d in range(1, 8)])
    for to in peers:
        pl.semaphore_signal(barrier, inc=1, device_id=to, device_id_type=MESH)

    for t in range(8):
        load_orb[t].wait()
        at = pl.ds(128 * t, 128)
        for r in range(8):
            hi, lo = split(orbv[t, pl.ds(r, 64, stride=8), :])
            amat[pl.ds(64 * r, 64), at] = hi
            amat[pl.ds(512 + 64 * r, 64), at] = lo

    def pick(b):
        at = pl.ds(pl.multiple_of(256 * b, 256), 256)
        hot = lax.broadcasted_iota(jnp.int32, (1024, 256), 0) == cols[:, at]
        res = jnp.dot(amat[...], jnp.where(hot, 1.0, 0.0).astype(BF), preferred_element_type=F32)
        here = rows[:, at] - 8 * g
        total = jnp.zeros((64, 256), F32)
        for r in range(8):
            part = res[64 * r:64 * r + 64] + res[512 + 64 * r:576 + 64 * r]
            total = total + jnp.where(here == r, part, 0.0)
        return jnp.concatenate([total[:, :128], total[:, 128:]], axis=0).T

    def inbound(d, part):
        return remote(
            columns((x + d) % 4, part), landing(part), in_s.at[part, d - 1], in_r.at[part, d - 1], xpeer(d))

    acopies = []
    for i in range(4):
        qa[i] = pick((1 - c) * 4 + (y + 1 + i) % 4)
        if i == 0:
            pl.semaphore_wait(barrier, len(peers))
            for d in (1, 3, 2):
                inbound(d, 0).start()
        acopies.append(remote(qa.at[i], ra.at[i], a_s.at[i], a_r.at[i], partner))
        acopies[i].start()
    bcopies = []
    for i in range(4):
        mine = pick(c * 4 + (y + 1 + i) % 4)
        acopies[i].wait_recv()
        qb[i] = mine + ra[i]
        if i < 3:
            bcopies.append(remote(qb.at[i], rb.at[i], b_s.at[i], b_r.at[i], ypeer(i + 1)))
            bcopies[i].start()

    def rearrange(start, stop):
        @pl.loop(start, stop)
        def _(n):
            at = pl.ds(pl.multiple_of(16 * n, 16), 16)
            v = vraw[at, :, :].astype(F32)
            vrow[:, at, :] = jnp.swapaxes(v, 0, 1).astype(BF)

    load_pot.wait()
    rearrange(0, 32)
    for cp in bcopies:
        cp.wait_recv()
    qc[...] = qb[3] + rb[0] + rb[1] + rb[2]
    ccopies = []
    for d in range(1, 8):
        to = (z + d) % 8
        ccopies.append(remote(qc.at[pl.ds(pl.multiple_of(16 * to, 16), 16), :], rc.at[d - 1],
                              c_s.at[d - 1], c_r.at[d - 1], zpeer(d)))
        ccopies[-1].start()
    rearrange(32, 64)
    total = qc[pl.ds(pl.multiple_of(16 * z, 16), 16), :]
    for d in range(1, 8):
        ccopies[d - 1].wait_recv()
        total = total + rc[d - 1]
    qd[...] = total
    dcopies = []
    for d in (1, 2, 3):
        dcopies.append(remote(qd, rd.at[d - 1], d_s.at[d - 1], d_r.at[d - 1], xpeer(d)))
        dcopies[-1].start()
    for d in (1, 3, 2):
        inbound(d, 1).start()
    rearrange(64, 80)
    for cp in dcopies:
        cp.wait_recv()
    lane = lax.broadcasted_iota(jnp.int32, (16, 128), 1)
    low = lane < 64
    halves = []
    for d in range(4):
        q = qd[...] if d == 0 else rd[d - 1]
        other = pltpu.roll(q, 64, 1)
        halves.append((jnp.where(low, q, other), jnp.where(low, other, q)))
    b = c * 4 + y
    for h in range(2):
        for t in range(2):
            v = jnp.zeros((16, 128), F32)
            for d in range(4):
                v = v + jnp.where(lane // 64 + 2 * t == (x + 4 - d) % 4, halves[d][h], 0.0)
            pt[2 * b + h, pl.ds(pl.multiple_of(16 * z, 16), 16), pl.ds(128 * t, 128)] = v

    def zpiece():
        return pt.at[pl.ds(2 * b, 2), pl.ds(pl.multiple_of(16 * z, 16), 16), :]

    zcopies = []
    for d in range(1, 8):
        zcopies.append(remote(zpiece(), zpiece(), z_s.at[d - 1], z_r.at[d - 1], zpeer(d)))
        zcopies[-1].start()
    rearrange(80, 112)
    for cp in zcopies:
        cp.wait_recv()

    def block(bb):
        return pt.at[pl.ds(2 * bb, 2)]

    ycopies, kcopies = [], []
    for d in (1, 3, 2):
        ycopies.append(remote(block(b), block(b), y_s.at[d - 1], y_r.at[d - 1], ypeer(d)))
        ycopies[-1].start()
    kcopies.append(remote(block(b), block(b), k_s.at[0], k_r.at[0], partner))
    kcopies[0].start()
    rearrange(112, 128)
    for cp in load_own:
        cp.wait()
    for part in range(2):
        for d in (1, 2, 3):
            inbound(d, part).wait_recv()
    for r in range(8):
        for t in range(2):
            hi, lo = split(orecv[t, pl.ds(r, 256, stride=8), :])
            ohi[r, :, pl.ds(128 * t, 128)] = hi
            olo[r, :, pl.ds(128 * t, 128)] = lo
    for n, d in enumerate((1, 3, 2)):
        ycopies[n].wait_recv()
        src = c * 4 + (y + 4 - d) % 4
        kcopies.append(remote(block(src), block(src), k_s.at[d], k_r.at[d], partner))
        kcopies[-1].start()
    for cp in kcopies:
        cp.wait_recv()

    eye = jnp.where(lax.broadcasted_iota(jnp.int32, (256, 256), 0)
                    == lax.broadcasted_iota(jnp.int32, (256, 256), 1), 1.0, 0.0).astype(BF)
    nt = (((1,), (1,)), ((), ()))
    for n in range(8):
        at = pl.ds(256 * n, 256)
        hi, lo = split(pt[2 * n:2 * n + 2].reshape(256, 256))
        pth[at, :] = hi
        ptl[at, :] = lo
        ph[:, at] = lax.dot_general(eye, hi, nt, preferred_element_type=F32).astype(BF)
        plo[:, at] = lax.dot_general(eye, lo, nt, preferred_element_type=F32).astype(BF)

    def outbound(r, d):
        to = (x + d) % 4
        return remote(
            ysend.at[r, pl.ds(pl.multiple_of(64 * to, 64), 64), :],
            y_out.at[r, :, pl.ds(pl.multiple_of(256 * x, 256), 256)],
            o_s.at[r, d - 1], o_r.at[r, d - 1], xpeer(d))

    def keep(r):
        return pltpu.make_async_copy(
            ysend.at[r, pl.ds(pl.multiple_of(64 * x, 64), 64), :],
            y_out.at[r, :, pl.ds(pl.multiple_of(256 * x, 256), 256)], o_l.at[r])

    @pl.loop(0, 8)
    def _(r):
        oh, ol = ohi[r], olo[r]
        acc = jnp.zeros((256, 256), F32)
        for n in range(2048 // MC):
            at = pl.ds(MC * n, MC)
            kern = (jnp.dot(pth[at, :], oh, preferred_element_type=F32)
                    + jnp.dot(ptl[at, :], oh, preferred_element_type=F32)
                    + jnp.dot(pth[at, :], ol, preferred_element_type=F32))
            wh, wl = split(kern * vrow[r, at, :].astype(F32))
            acc = (acc + jnp.dot(ph[:, at], wh, preferred_element_type=F32)
                   + jnp.dot(plo[:, at], wh, preferred_element_type=F32)
                   + jnp.dot(ph[:, at], wl, preferred_element_type=F32))
        ysend[r] = -acc
        for d in (1, 3, 2):
            outbound(r, d).start()
        keep(r).start()

    for part in range(2):
        for d in (1, 2, 3):
            inbound(d, part).wait_send()
    for cp in acopies + bcopies + ccopies + dcopies + zcopies + ycopies + kcopies:
        cp.wait_send()

    @pl.loop(0, 8)
    def _(r):
        for d in (1, 3, 2):
            outbound(r, d).wait()
        keep(r).wait()


def local(orbitals, potentials, point_rows, point_cols):
    vm, dma = pltpu.VMEM, pltpu.SemaphoreType.DMA
    hbm = pl.BlockSpec(memory_space=pl.ANY)
    ix = pl.BlockSpec(memory_space=pltpu.VMEM)
    scratch = [
        vm((8, 512, 128), F32), vm((2048, 8, 256), BF), vm((8, 2048, 256), BF),
        vm((1024, 1024), BF), vm((2, 2048, 128), F32), vm((8, 256, 256), BF), vm((8, 256, 256), BF),
        vm((4, 128, 128), F32), vm((4, 128, 128), F32), vm((4, 128, 128), F32), vm((3, 128, 128), F32),
        vm((128, 128), F32), vm((7, 16, 128), F32), vm((16, 128), F32), vm((3, 16, 128), F32),
        vm((16, 128, 256), F32), vm((2048, 256), BF), vm((2048, 256), BF),
        vm((256, 2048), BF), vm((256, 2048), BF), vm((8, 256, 256), F32),
        dma((11,)), dma((2, 3)), dma((2, 3)), dma((4,)), dma((4,)), dma((3,)), dma((3,)),
        dma((7,)), dma((7,)), dma((3,)), dma((3,)), dma((7,)), dma((7,)), dma((3,)), dma((3,)),
        dma((4,)), dma((4,)), dma((8, 3)), dma((8, 3)), dma((8,)),
    ]
    out = pl.pallas_call(
        body,
        out_shape=jax.ShapeDtypeStruct((8, 64, 1024), F32),
        in_specs=[hbm, hbm, ix, ix],
        out_specs=hbm,
        scratch_shapes=scratch,
        compiler_params=pltpu.CompilerParams(
            collective_id=0, has_side_effects=True, vmem_limit_bytes=60 * 1024 * 1024),
        name="exchange",
    )(orbitals.reshape(512, 1024), potentials, point_rows.reshape(1, -1), point_cols.reshape(1, -1))
    return jnp.transpose(out, (1, 0, 2))


def solution(mesh):
    in_specs = (P("band", "grid", None), P(None, "grid", "band"), P(), P())
    out_specs = P("band", "grid", None)
    return jax.shard_map(local, mesh=mesh, in_specs=in_specs, out_specs=out_specs, check_vma=False)
```

time: 436 us -> 82.7 us (0.19)
  the two profiles are of different devices: /device:TPU:8 before, /device:TPU:1 now
where the time goes in v1:
time: 82.7 us; the launch traced here: 82.5 us
  Pallas kernels  78.3 us (95%)
  local copies, waits for them, and re-layouts  4.13 us (5%)
    pallas_call x1, Pallas kernels, local(): pl.pallas_call(body, out_shape=jax.ShapeDtypeStruct((8, 64, 1024), F32),...  78.3 us
    transpose x1, local copies, waits for them, and re-layouts, local(): return jnp.transpose(out, (1, 0, 2))  4.13 us

profile of v1, /device:TPU:1, one launch (start us, length us, event | category | flops | bytes accessed | tf_op | source)
XLA Modules:
  0.0 82.5 jit_solution(341715907135025214)
XLA Ops:
  0.0 78.3 %exchange.1 = f32[8,64,1024]{2,1,0:T(8,128)} custom-call(f32[512,1024]{1,0:T(8,128)} %bitcast.5, bf16[2048,8,256]{2,1,0:T(8,128)(2,1)} %pot.1, s32[1,2048]{1,0:T(1,128)} %bitcast.6, s32[1,2048]{1,0:T(1,128)} %bitcast.7), custom_call_target="tpu_custom_call" | custom-call | tf_op jit(solution)/shard_map/exchange/pallas_call | solution.py:267
  78.3 4.1 %copy.5 = f32[64,8,1024]{2,1,0:T(8,128)} copy(f32[64,8,1024]{2,0,1:T(8,128)} %bitcast.4) | data formatting | bytes 4194304 | tf_op jit(solution)/shard_map/transpose | solution.py:277

commit v2 on v1

v2 whole, which is shorter than its diff:
```python
import jax
import jax.numpy as jnp
from jax import lax
from jax.experimental import pallas as pl
from jax.experimental.pallas import tpu as pltpu
from jax.sharding import PartitionSpec as P

MESH = pl.DeviceIdType.MESH
BF = jnp.bfloat16
F32 = jnp.float32
MC = 512
R1, R2 = 32, 96
LAG = 3
ORDER = (0, 1, 7, 2, 6, 3, 5, 4)
GREET = 3
IN_FIRST, IN_LAST = range(4), range(4, 8)


def split(v):
    hi = v.astype(BF)
    return hi, (v - hi.astype(F32)).astype(BF)


def body(orb, pot, rows, cols, y_out,
         orbv, vraw, vrow, amat, orecv, ohi, olo, qa, ra, qb, rb, qc, rc,
         blk, pth, ptl, ph, plo, ysend,
         lsem, in_s, in_r, a_s, a_r, b_s, b_r, c_s, c_r, d_s, d_r,
         y_s, y_r, e_s, e_r, k_s, k_r, o_s, o_r, o_l):
    x = lax.axis_index("band")
    g = lax.axis_index("grid")
    z, y, c = g // 8, (g // 2) % 4, g % 2

    def dev(xx, zz, yy, cc):
        return (xx, (zz * 4 + yy) * 2 + cc)

    def xpeer(d):
        return dev((x + d) % 4, z, y, c)

    def zpeer(d):
        return dev(x, (z + d) % 8, y, c)

    def ypeer(d):
        return dev(x, z, (y + d) % 4, c)

    partner = dev(x, z, y, 1 - c)

    def remote(src, dst, ss, rs, to):
        return pltpu.make_async_remote_copy(
            src_ref=src, dst_ref=dst, send_sem=ss, recv_sem=rs,
            device_id=to, device_id_type=MESH)

    load_orb = [pltpu.make_async_copy(orb.at[:, pl.ds(128 * t, 128)], orbv.at[t], lsem.at[t])
                for t in range(8)]
    for cp in load_orb:
        cp.start()
    load_pot = pltpu.make_async_copy(pot, vraw, lsem.at[10])
    load_pot.start()

    load_own = [pltpu.make_async_copy(
        orb.at[:, pl.ds(pl.multiple_of(256 * x + 128 * t, 128), 128)],
        orecv.at[t, pl.ds(pl.multiple_of(512 * x, 512), 512), :], lsem.at[8 + t]) for t in range(2)]
    for cp in load_own:
        cp.start()

    barrier = pltpu.get_barrier_semaphore()
    peers = ([partner] + [ypeer(d) for d in (1, 2, 3)]
             + [dev((x + dx) % 4, (z + dz) % 8, y, c) for dz in range(8) for dx in range(4) if dz or dx])
    for to in peers:
        pl.semaphore_signal(barrier, inc=1, device_id=to, device_id_type=MESH)

    for t in range(8):
        load_orb[t].wait()
        at = pl.ds(128 * t, 128)
        for r in range(8):
            hi, lo = split(orbv[t, pl.ds(r, 64, stride=8), :])
            amat[pl.ds(64 * r, 64), at] = hi
            amat[pl.ds(512 + 64 * r, 64), at] = lo

    def pick(b):
        at = pl.ds(pl.multiple_of(256 * b, 256), 256)
        hot = lax.broadcasted_iota(jnp.int32, (1024, 256), 0) == cols[:, at]
        res = jnp.dot(amat[...], jnp.where(hot, 1.0, 0.0).astype(BF), preferred_element_type=F32)
        here = rows[:, at] - 8 * g
        total = jnp.zeros((64, 256), F32)
        for r in range(8):
            part = res[64 * r:64 * r + 64] + res[512 + 64 * r:576 + 64 * r]
            total = total + jnp.where(here == r, part, 0.0)
        return jnp.concatenate([total[:, :128], total[:, 128:]], axis=0).T

    def inbound(d, part):
        t, piece = part // 4, part % 4
        to = (x + d) % 4
        return remote(
            orb.at[pl.ds(128 * piece, 128), pl.ds(pl.multiple_of(256 * to + 128 * t, 128), 128)],
            orecv.at[t, pl.ds(pl.multiple_of(512 * x + 128 * piece, 128), 128), :],
            in_s.at[part, d - 1], in_r.at[part, d - 1], xpeer(d))

    def send_inbound(parts):
        for part in parts:
            for d in (1, 3, 2):
                inbound(d, part).start()

    pend = []

    def go(cp):
        cp.start()
        pend.append(cp)
        return cp

    def rearrange(start, stop):
        @pl.loop(start, stop)
        def _(n):
            at = pl.ds(pl.multiple_of(16 * n, 16), 16)
            v = vraw[at, :, :].astype(F32)
            vrow[:, at, :] = jnp.swapaxes(v, 0, 1).astype(BF)

    acopies = []
    for i in range(4):
        qa[i] = pick((1 - c) * 4 + (y + 1 + i) % 4)
        if i == GREET:
            pl.semaphore_wait(barrier, len(peers))
            send_inbound(IN_FIRST)
        if i >= GREET:
            for k in range(len(acopies), i + 1):
                acopies.append(go(remote(qa.at[k], ra.at[k], a_s.at[k], a_r.at[k], partner)))
    bcopies = []
    for i in range(4):
        mine = pick(c * 4 + (y + 1 + i) % 4)
        acopies[i].wait_recv()
        qb[i] = mine + ra[i]
        if i < 3:
            bcopies.append(go(remote(qb.at[i], rb.at[i], b_s.at[i], b_r.at[i], ypeer(i + 1))))
    load_pot.wait()
    rearrange(0, R1)
    for cp in bcopies:
        cp.wait_recv()
    qc[...] = qb[3] + rb[0] + rb[1] + rb[2]
    ccopies = []
    for d in (4, 3, 5, 2, 6, 1, 7):
        to = (z + d) % 8
        ccopies.append(go(remote(qc.at[pl.ds(pl.multiple_of(16 * to, 16), 16), :], rc.at[d - 1],
                                 c_s.at[d - 1], c_r.at[d - 1], zpeer(d))))
    rearrange(R1, R2)
    total = qc[pl.ds(pl.multiple_of(16 * z, 16), 16), :]
    for cp in ccopies:
        cp.wait_recv()
    for d in range(7):
        total = total + rc[d]

    b = c * 4 + y
    blk[b, x, pl.ds(pl.multiple_of(16 * z, 16), 16), :] = total
    order = ORDER
    piece = blk.at[b, x, pl.ds(pl.multiple_of(16 * z, 16), 16), :]
    dcopies = {}
    for dz in order:
        for dx in (1, 3, 2, 0):
            if dz or dx:
                dcopies[dz, dx] = go(remote(piece, piece, d_s.at[dz, dx], d_r.at[dz, dx],
                                            dev((x + dx) % 4, (z + dz) % 8, y, c)))
    send_inbound(IN_LAST)
    rearrange(R2, 128)

    def group(dy, dz):
        return blk.at[c * 4 + (y + dy + 4) % 4, :,
                      pl.ds(pl.multiple_of(16 * ((z + 8 - dz) % 8), 16), 16), :]

    def cross(dy, dz):
        src = group(dy, dz)
        return go(remote(src, src, k_s.at[dy % 4, dz], k_r.at[dy % 4, dz], partner))

    up, down, relay, kcopies = {}, {}, {}, {}
    for k in range(8 + 2 * LAG):
        if k < 8:
            dz = order[k]
            for dx in range(4):
                if dz or dx:
                    dcopies[dz, dx].wait_recv()
            src = group(0, dz)
            up[dz] = go(remote(src, src, y_s.at[0, dz], y_r.at[0, dz], ypeer(1)))
            down[dz] = go(remote(src, src, y_s.at[1, dz], y_r.at[1, dz], ypeer(3)))
            kcopies[0, dz] = cross(0, dz)
        if 0 <= k - LAG < 8:
            dz = order[k - LAG]
            up[dz].wait_recv()
            if (k - LAG) % 2 == 0:
                src = group(-1, dz)
                relay[dz] = go(remote(src, src, e_s.at[dz], e_r.at[dz], ypeer(1)))
            kcopies[3, dz] = cross(-1, dz)
            down[dz].wait_recv()
            if (k - LAG) % 2 == 1:
                src = group(1, dz)
                relay[dz] = go(remote(src, src, e_s.at[dz], e_r.at[dz], ypeer(3)))
            kcopies[1, dz] = cross(1, dz)
        if 0 <= k - 2 * LAG < 8:
            dz = order[k - 2 * LAG]
            relay[dz].wait_recv()
            kcopies[2, dz] = cross(2, dz)

    for cp in load_own:
        cp.wait()
    for part in range(8):
        for d in (1, 2, 3):
            inbound(d, part).wait_recv()
    for r in range(8):
        for t in range(2):
            hi, lo = split(orecv[t, pl.ds(r, 256, stride=8), :])
            ohi[r, :, pl.ds(128 * t, 128)] = hi
            olo[r, :, pl.ds(128 * t, 128)] = lo

    eye = jnp.where(lax.broadcasted_iota(jnp.int32, (256, 256), 0)
                    == lax.broadcasted_iota(jnp.int32, (256, 256), 1), 1.0, 0.0).astype(BF)
    nt = (((1,), (1,)), ((), ()))
    low = lax.broadcasted_iota(jnp.int32, (128, 128), 1) < 64

    def unpack(n):
        first, second = [], []
        for t in range(2):
            even, odd = blk[n, 2 * t], blk[n, 2 * t + 1]
            first.append(jnp.where(low, even, pltpu.roll(odd, 64, 1)))
            second.append(jnp.where(low, pltpu.roll(even, 64, 1), odd))
        full = jnp.concatenate([jnp.concatenate(first, axis=1), jnp.concatenate(second, axis=1)], axis=0)
        at = pl.ds(pl.multiple_of(256 * n, 256), 256)
        hi, lo = split(full)
        pth[at, :] = hi
        ptl[at, :] = lo
        ph[:, at] = lax.dot_general(eye, hi, nt, preferred_element_type=F32).astype(BF)
        plo[:, at] = lax.dot_general(eye, lo, nt, preferred_element_type=F32).astype(BF)

    def outbound(r, d):
        to = (x + d) % 4
        return remote(
            ysend.at[r, pl.ds(pl.multiple_of(64 * to, 64), 64), :],
            y_out.at[r, :, pl.ds(pl.multiple_of(256 * x, 256), 256)],
            o_s.at[r, d - 1], o_r.at[r, d - 1], xpeer(d))

    def keep(r):
        return pltpu.make_async_copy(
            ysend.at[r, pl.ds(pl.multiple_of(64 * x, 64), 64), :],
            y_out.at[r, :, pl.ds(pl.multiple_of(256 * x, 256), 256)], o_l.at[r])

    def half(r, side, acc):
        oh, ol = ohi[r], olo[r]
        for n in range(1024 // MC):
            at = pl.ds(pl.multiple_of(1024 * side + MC * n, MC), MC)
            kern = (jnp.dot(pth[at, :], oh, preferred_element_type=F32)
                    + jnp.dot(ptl[at, :], oh, preferred_element_type=F32)
                    + jnp.dot(pth[at, :], ol, preferred_element_type=F32))
            wh, wl = split(kern * vrow[r, at, :].astype(F32))
            acc = (acc + jnp.dot(ph[:, at], wh, preferred_element_type=F32)
                   + jnp.dot(plo[:, at], wh, preferred_element_type=F32)
                   + jnp.dot(ph[:, at], wl, preferred_element_type=F32))
        return acc

    def finish(r, acc):
        ysend[r] = -acc
        for d in (1, 3, 2):
            outbound(r, d).start()
        keep(r).start()

    zero = jnp.zeros((256, 256), F32)
    for dy in range(4):
        unpack(c * 4 + (y + dy) % 4)
    ysend[0] = half(0, c, zero)
    for dy in (0, 1, 3, 2):
        for dz in order:
            kcopies[dy, dz].wait_recv()
        unpack((1 - c) * 4 + (y + dy) % 4)
    finish(0, half(0, 1 - c, ysend[0]))

    @pl.loop(1, 8)
    def _(r):
        finish(r, half(r, 1, half(r, 0, zero)))

    for part in range(8):
        for d in (1, 2, 3):
            inbound(d, part).wait_send()
    for cp in pend:
        cp.wait_send()

    @pl.loop(0, 8)
    def _(r):
        for d in (1, 3, 2):
            outbound(r, d).wait()
        keep(r).wait()


def relayout(src, dst):
    dst[...] = jnp.swapaxes(src[...], 0, 1)


def local(orbitals, potentials, point_rows, point_cols):
    vm, dma = pltpu.VMEM, pltpu.SemaphoreType.DMA
    hbm = pl.BlockSpec(memory_space=pl.ANY)
    ix = pl.BlockSpec(memory_space=pltpu.VMEM)
    scratch = [
        vm((8, 512, 128), F32), vm((2048, 8, 256), BF), vm((8, 2048, 256), BF),
        vm((1024, 1024), BF), vm((2, 2048, 128), F32), vm((8, 256, 256), BF), vm((8, 256, 256), BF),
        vm((4, 128, 128), F32), vm((4, 128, 128), F32), vm((4, 128, 128), F32), vm((3, 128, 128), F32),
        vm((128, 128), F32), vm((7, 16, 128), F32), vm((8, 4, 128, 128), F32),
        vm((2048, 256), BF), vm((2048, 256), BF),
        vm((256, 2048), BF), vm((256, 2048), BF), vm((8, 256, 256), F32),
        dma((11,)), dma((8, 3)), dma((8, 3)), dma((4,)), dma((4,)), dma((3,)), dma((3,)),
        dma((7,)), dma((7,)), dma((8, 4)), dma((8, 4)), dma((2, 8)), dma((2, 8)), dma((8,)), dma((8,)),
        dma((4, 8)), dma((4, 8)), dma((8, 3)), dma((8, 3)), dma((8,)),
    ]
    out = pl.pallas_call(
        body,
        out_shape=jax.ShapeDtypeStruct((8, 64, 1024), F32),
        in_specs=[hbm, hbm, ix, ix],
        out_specs=hbm,
        scratch_shapes=scratch,
        compiler_params=pltpu.CompilerParams(
            collective_id=0, has_side_effects=True, vmem_limit_bytes=60 * 1024 * 1024),
        name="exchange",
    )(orbitals.reshape(512, 1024), potentials, point_rows.reshape(1, -1), point_cols.reshape(1, -1))
    return pl.pallas_call(
        relayout,
        out_shape=jax.ShapeDtypeStruct((64, 8, 1024), F32),
        grid=(4,),
        in_specs=[pl.BlockSpec((8, 16, 1024), lambda i: (0, i, 0))],
        out_specs=pl.BlockSpec((16, 8, 1024), lambda i: (i, 0, 0)),
        name="relayout",
    )(out)


def solution(mesh):
    in_specs = (P("band", "grid", None), P(None, "grid", "band"), P(), P())
    out_specs = P("band", "grid", None)
    return jax.shard_map(local, mesh=mesh, in_specs=in_specs, out_specs=out_specs, check_vma=False)
```

time: 82.7 us -> 76.7 us (0.927)
  the two profiles are of different devices: /device:TPU:1 before, /device:TPU:8 now
where the time goes in v2:
time: 76.7 us; the launch traced here: 76.5 us
  Pallas kernels  76.5 us (100%)
    pallas_call x1, Pallas kernels, local(): pl.pallas_call(body, out_shape=jax.ShapeDtypeStruct((8, 64, 1024), F32),...  72.6 us
    pallas_call x1, Pallas kernels, local(): pl.pallas_call(relayout, out_shape=jax.ShapeDtypeStruct((64, 8, 1024), F3...  3.92 us

profile of v2, /device:TPU:8, one launch (start us, length us, event | category | flops | bytes accessed | tf_op | source)
XLA Modules:
  0.0 76.5 jit_solution(5592503565860859066)
XLA Ops:
  0.0 72.6 %exchange.1.src = f32[8,64,1024]{2,1,0:T(8,128)} custom-call(f32[512,1024]{1,0:T(8,128)} %bitcast.3, bf16[2048,8,256]{2,1,0:T(8,128)(2,1)} %pot.1, s32[1,2048]{1,0:T(1,128)} %bitcast.4, s32[1,2048]{1,0:T(1,128)} %bitcast.5), custom_call_target="tpu_custom_call" | custom-call | tf_op jit(solution)/shard_map/exchange/pallas_call | solution.py:306
  72.6 3.9 %relayout.1 = f32[64,8,1024]{2,1,0:T(8,128)} custom-call(f32[8,64,1024]{2,1,0:T(8,128)} %exchange.1.src), custom_call_target="tpu_custom_call" | custom-call | tf_op jit(solution)/shard_map/relayout/pallas_call | solution.py:316

commit v3 on v2

--- a/solution.py
+++ b/solution.py
@@ -9,9 +9,10 @@
 BF = jnp.bfloat16
 F32 = jnp.float32
 MC = 512
-R1, R2 = 32, 96
-LAG = 3
-ORDER = (0, 1, 7, 2, 6, 3, 5, 4)
+R1, R2 = 32, 64
+PASSED = {2: (0,), 6: (1,), 4: (2, 3)}
+LAG = 4
+ORDER = (0, 1, 7, 3, 5, 2, 6, 4)
 GREET = 3
 IN_FIRST, IN_LAST = range(4), range(4, 8)
 
@@ -25,7 +26,7 @@
          orbv, vraw, vrow, amat, orecv, ohi, olo, qa, ra, qb, rb, qc, rc,
          blk, pth, ptl, ph, plo, ysend,
          lsem, in_s, in_r, a_s, a_r, b_s, b_r, c_s, c_r, d_s, d_r,
-         y_s, y_r, e_s, e_r, k_s, k_r, o_s, o_r, o_l):
+         p_s, p_r, y_s, y_r, e_s, e_r, k_s, k_r, o_s, o_r, o_l):
     x = lax.axis_index("band")
     g = lax.axis_index("grid")
     z, y, c = g // 8, (g // 2) % 4, g % 2
@@ -64,7 +65,8 @@
 
     barrier = pltpu.get_barrier_semaphore()
     peers = ([partner] + [ypeer(d) for d in (1, 2, 3)]
-             + [dev((x + dx) % 4, (z + dz) % 8, y, c) for dz in range(8) for dx in range(4) if dz or dx])
+             + [dev((x + dx) % 4, (z + dz) % 8, y, c) for dz in range(8) for dx in range(4)
+                if (dz or dx) and (dz in (0, 1, 3, 5, 7) or dx == 0)])
     for to in peers:
         pl.semaphore_signal(barrier, inc=1, device_id=to, device_id_type=MESH)
 
@@ -152,7 +154,7 @@
     order = ORDER
     piece = blk.at[b, x, pl.ds(pl.multiple_of(16 * z, 16), 16), :]
     dcopies = {}
-    for dz in order:
+    for dz in (0, 1, 7, 3, 5):
         for dx in (1, 3, 2, 0):
             if dz or dx:
                 dcopies[dz, dx] = go(remote(piece, piece, d_s.at[dz, dx], d_r.at[dz, dx],
@@ -168,14 +170,25 @@
         src = group(dy, dz)
         return go(remote(src, src, k_s.at[dy % 4, dz], k_r.at[dy % 4, dz], partner))
 
-    up, down, relay, kcopies = {}, {}, {}, {}
+    up, down, relay, kcopies, passed = {}, {}, {}, {}, {}
     for k in range(8 + 2 * LAG):
         if k < 8:
             dz = order[k]
-            for dx in range(4):
-                if dz or dx:
-                    dcopies[dz, dx].wait_recv()
             src = group(0, dz)
+            if dz in (0, 1, 3, 5, 7):
+                for dx in range(4):
+                    if dz or dx:
+                        dcopies[dz, dx].wait_recv()
+            else:
+                for n in PASSED[dz]:
+                    passed[n].wait_recv()
+            if dz in (1, 7):
+                n = 0 if dz == 1 else 1
+                passed[n] = go(remote(src, src, p_s.at[n], p_r.at[n], zpeer(dz)))
+            if dz in (3, 5):
+                n = 2 if dz == 3 else 3
+                part = src.at[pl.ds(2 * (n - 2), 2)]
+                passed[n] = go(remote(part, part, p_s.at[n], p_r.at[n], zpeer(1 if dz == 3 else 7)))
             up[dz] = go(remote(src, src, y_s.at[0, dz], y_r.at[0, dz], ypeer(1)))
             down[dz] = go(remote(src, src, y_s.at[1, dz], y_r.at[1, dz], ypeer(3)))
             kcopies[0, dz] = cross(0, dz)
@@ -284,8 +297,17 @@
         keep(r).wait()
 
 
-def relayout(src, dst):
-    dst[...] = jnp.swapaxes(src[...], 0, 1)
+def relayout(src, dst, got, done, s_in, s_out):
+    ins = [pltpu.make_async_copy(src.at[:, pl.ds(8 * i, 8), :], got.at[i], s_in.at[i]) for i in range(8)]
+    outs = [pltpu.make_async_copy(done.at[i], dst.at[pl.ds(8 * i, 8)], s_out.at[i]) for i in range(8)]
+    for cp in ins:
+        cp.start()
+    for i in range(8):
+        ins[i].wait()
+        done[i] = jnp.swapaxes(got[i], 0, 1)
+        outs[i].start()
+    for cp in outs:
+        cp.wait()
 
 
 def local(orbitals, potentials, point_rows, point_cols):
@@ -300,7 +322,7 @@
         vm((2048, 256), BF), vm((2048, 256), BF),
         vm((256, 2048), BF), vm((256, 2048), BF), vm((8, 256, 256), F32),
         dma((11,)), dma((8, 3)), dma((8, 3)), dma((4,)), dma((4,)), dma((3,)), dma((3,)),
-        dma((7,)), dma((7,)), dma((8, 4)), dma((8, 4)), dma((2, 8)), dma((2, 8)), dma((8,)), dma((8,)),
+        dma((7,)), dma((7,)), dma((8, 4)), dma((8, 4)), dma((4,)), dma((4,)), dma((2, 8)), dma((2, 8)), dma((8,)), dma((8,)),
         dma((4, 8)), dma((4, 8)), dma((8, 3)), dma((8, 3)), dma((8,)),
     ]
     out = pl.pallas_call(
@@ -316,9 +338,10 @@
     return pl.pallas_call(
         relayout,
         out_shape=jax.ShapeDtypeStruct((64, 8, 1024), F32),
-        grid=(4,),
-        in_specs=[pl.BlockSpec((8, 16, 1024), lambda i: (0, i, 0))],
-        out_specs=pl.BlockSpec((16, 8, 1024), lambda i: (i, 0, 0)),
+        in_specs=[hbm],
+        out_specs=hbm,
+        scratch_shapes=[vm((8, 8, 8, 1024), F32), vm((8, 8, 8, 1024), F32), dma((8,)), dma((8,))],
+        compiler_params=pltpu.CompilerParams(vmem_limit_bytes=60 * 1024 * 1024),
         name="relayout",
     )(out)
 

time: 76.7 us -> 73.6 us (0.960)
  Pallas kernels: 76.5 us -> 73.2 us
    pallas_call x1, Pallas kernels: 72.6 us -> 70.7 us  [local(): pl.pallas_call(body, out_shape=jax.ShapeDtypeStruct((8, 64, 1024), F32),...]
    pallas_call x1, Pallas kernels: 3.92 us -> 2.44 us  [local(): pl.pallas_call(relayout, out_shape=jax.ShapeDtypeStruct((64, 8, 1024), F3...]
where the time goes in v3:
time: 73.6 us; the launch traced here: 73.3 us
  Pallas kernels  73.2 us (99%)
    pallas_call x1, Pallas kernels, local(): pl.pallas_call(body, out_shape=jax.ShapeDtypeStruct((8, 64, 1024), F32),...  70.7 us
    pallas_call x1, Pallas kernels, local(): pl.pallas_call(relayout, out_shape=jax.ShapeDtypeStruct((64, 8, 1024), F3...  2.44 us

profile of v3, /device:TPU:8, one launch (start us, length us, event | category | flops | bytes accessed | tf_op | source)
XLA Modules:
  0.0 73.3 jit_solution(7978020133504250227)
XLA Ops:
  0.0 70.7 %exchange.1.src = f32[8,64,1024]{2,1,0:T(8,128)} custom-call(f32[512,1024]{1,0:T(8,128)} %bitcast.3, bf16[2048,8,256]{2,1,0:T(8,128)(2,1)} %pot.1, s32[1,2048]{1,0:T(1,128)} %bitcast.4, s32[1,2048]{1,0:T(1,128)} %bitcast.5), custom_call_target="tpu_custom_call" | custom-call | tf_op jit(solution)/shard_map/exchange/pallas_call | solution.py:328
  70.7 2.4 %relayout.1 = f32[64,8,1024]{2,1,0:T(8,128)} custom-call(f32[8,64,1024]{2,1,0:T(8,128)} %exchange.1.src), custom_call_target="tpu_custom_call" | custom-call | tf_op jit(solution)/shard_map/relayout/pallas_call | solution.py:338

commit v4 on v3

--- a/solution.py
+++ b/solution.py
@@ -169,6 +169,53 @@
     def cross(dy, dz):
         src = group(dy, dz)
         return go(remote(src, src, k_s.at[dy % 4, dz], k_r.at[dy % 4, dz], partner))
+
+    eye = jnp.where(lax.broadcasted_iota(jnp.int32, (256, 256), 0)
+                    == lax.broadcasted_iota(jnp.int32, (256, 256), 1), 1.0, 0.0).astype(BF)
+    nt = (((1,), (1,)), ((), ()))
+    low = lax.broadcasted_iota(jnp.int32, (128, 128), 1) < 64
+
+    def unpack(n):
+        first, second = [], []
+        for t in range(2):
+            even, odd = blk[n, 2 * t], blk[n, 2 * t + 1]
+            first.append(jnp.where(low, even, pltpu.roll(odd, 64, 1)))
+            second.append(jnp.where(low, pltpu.roll(even, 64, 1), odd))
+        full = jnp.concatenate([jnp.concatenate(first, axis=1), jnp.concatenate(second, axis=1)], axis=0)
+        at = pl.ds(pl.multiple_of(256 * n, 256), 256)
+        hi, lo = split(full)
+        pth[at, :] = hi
+        ptl[at, :] = lo
+        ph[:, at] = lax.dot_general(eye, hi, nt, preferred_element_type=F32).astype(BF)
+        plo[:, at] = lax.dot_general(eye, lo, nt, preferred_element_type=F32).astype(BF)
+
+    def contrib(r, start, size, acc):
+        oh, ol = ohi[r], olo[r]
+        at = pl.ds(pl.multiple_of(start, size), size)
+        kern = (jnp.dot(pth[at, :], oh, preferred_element_type=F32)
+                + jnp.dot(ptl[at, :], oh, preferred_element_type=F32)
+                + jnp.dot(pth[at, :], ol, preferred_element_type=F32))
+        wh, wl = split(kern * vrow[r, at, :].astype(F32))
+        return (acc + jnp.dot(ph[:, at], wh, preferred_element_type=F32)
+                + jnp.dot(plo[:, at], wh, preferred_element_type=F32)
+                + jnp.dot(ph[:, at], wl, preferred_element_type=F32))
+
+    def first(n):
+        unpack(n)
+        ysend[0] = contrib(0, 256 * n, 256, ysend[0])
+
+    def split_inbound(t):
+        load_own[t].wait()
+        for part in range(4 * t, 4 * t + 4):
+            for d in (1, 2, 3):
+                inbound(d, part).wait_recv()
+        for r in range(8):
+            hi, lo = split(orecv[t, pl.ds(r, 256, stride=8), :])
+            ohi[r, :, pl.ds(128 * t, 128)] = hi
+            olo[r, :, pl.ds(128 * t, 128)] = lo
+
+    split_inbound(0)
+    ysend[0] = jnp.zeros((256, 256), F32)
 
     up, down, relay, kcopies, passed = {}, {}, {}, {}, {}
     for k in range(8 + 2 * LAG):
@@ -208,36 +255,10 @@
             dz = order[k - 2 * LAG]
             relay[dz].wait_recv()
             kcopies[2, dz] = cross(2, dz)
-
-    for cp in load_own:
-        cp.wait()
-    for part in range(8):
-        for d in (1, 2, 3):
-            inbound(d, part).wait_recv()
-    for r in range(8):
-        for t in range(2):
-            hi, lo = split(orecv[t, pl.ds(r, 256, stride=8), :])
-            ohi[r, :, pl.ds(128 * t, 128)] = hi
-            olo[r, :, pl.ds(128 * t, 128)] = lo
-
-    eye = jnp.where(lax.broadcasted_iota(jnp.int32, (256, 256), 0)
-                    == lax.broadcasted_iota(jnp.int32, (256, 256), 1), 1.0, 0.0).astype(BF)
-    nt = (((1,), (1,)), ((), ()))
-    low = lax.broadcasted_iota(jnp.int32, (128, 128), 1) < 64
-
-    def unpack(n):
-        first, second = [], []
-        for t in range(2):
-            even, odd = blk[n, 2 * t], blk[n, 2 * t + 1]
-            first.append(jnp.where(low, even, pltpu.roll(odd, 64, 1)))
-            second.append(jnp.where(low, pltpu.roll(even, 64, 1), odd))
-        full = jnp.concatenate([jnp.concatenate(first, axis=1), jnp.concatenate(second, axis=1)], axis=0)
-        at = pl.ds(pl.multiple_of(256 * n, 256), 256)
-        hi, lo = split(full)
-        pth[at, :] = hi
-        ptl[at, :] = lo
-        ph[:, at] = lax.dot_general(eye, hi, nt, preferred_element_type=F32).astype(BF)
-        plo[:, at] = lax.dot_general(eye, lo, nt, preferred_element_type=F32).astype(BF)
+        if k == 7 + 2 * LAG:
+            split_inbound(1)
+            for dy in (0, 1, 3):
+                first(c * 4 + (y + dy) % 4)
 
     def outbound(r, d):
         to = (x + d) % 4
@@ -251,38 +272,25 @@
             ysend.at[r, pl.ds(pl.multiple_of(64 * x, 64), 64), :],
             y_out.at[r, :, pl.ds(pl.multiple_of(256 * x, 256), 256)], o_l.at[r])
 
-    def half(r, side, acc):
-        oh, ol = ohi[r], olo[r]
-        for n in range(1024 // MC):
-            at = pl.ds(pl.multiple_of(1024 * side + MC * n, MC), MC)
-            kern = (jnp.dot(pth[at, :], oh, preferred_element_type=F32)
-                    + jnp.dot(ptl[at, :], oh, preferred_element_type=F32)
-                    + jnp.dot(pth[at, :], ol, preferred_element_type=F32))
-            wh, wl = split(kern * vrow[r, at, :].astype(F32))
-            acc = (acc + jnp.dot(ph[:, at], wh, preferred_element_type=F32)
-                   + jnp.dot(plo[:, at], wh, preferred_element_type=F32)
-                   + jnp.dot(ph[:, at], wl, preferred_element_type=F32))
-        return acc
-
     def finish(r, acc):
         ysend[r] = -acc
         for d in (1, 3, 2):
             outbound(r, d).start()
         keep(r).start()
 
-    zero = jnp.zeros((256, 256), F32)
-    for dy in range(4):
-        unpack(c * 4 + (y + dy) % 4)
-    ysend[0] = half(0, c, zero)
+    first(c * 4 + (y + 2) % 4)
     for dy in (0, 1, 3, 2):
         for dz in order:
             kcopies[dy, dz].wait_recv()
-        unpack((1 - c) * 4 + (y + dy) % 4)
-    finish(0, half(0, 1 - c, ysend[0]))
+        first((1 - c) * 4 + (y + dy) % 4)
+    finish(0, ysend[0])
 
     @pl.loop(1, 8)
     def _(r):
-        finish(r, half(r, 1, half(r, 0, zero)))
+        acc = jnp.zeros((256, 256), F32)
+        for n in range(2048 // MC):
+            acc = contrib(r, MC * n, MC, acc)
+        finish(r, acc)
 
     for part in range(8):
         for d in (1, 2, 3):

time: 73.6 us -> 73.5 us (level)
  no operation moved by 1% of the time
where the time goes in v4:
time: 73.5 us; the launch traced here: 73.3 us
  Pallas kernels  73.1 us (99%)
    pallas_call x1, Pallas kernels, local(): pl.pallas_call(body, out_shape=jax.ShapeDtypeStruct((8, 64, 1024), F32),...  70.7 us
    pallas_call x1, Pallas kernels, local(): pl.pallas_call(relayout, out_shape=jax.ShapeDtypeStruct((64, 8, 1024), F3...  2.44 us

profile of v4, /device:TPU:8, one launch (start us, length us, event | category | flops | bytes accessed | tf_op | source)
XLA Modules:
  0.0 73.3 jit_solution(5901857663563137431)
XLA Ops:
  0.0 70.7 %exchange.1.src = f32[8,64,1024]{2,1,0:T(8,128)} custom-call(f32[512,1024]{1,0:T(8,128)} %bitcast.3, bf16[2048,8,256]{2,1,0:T(8,128)(2,1)} %pot.1, s32[1,2048]{1,0:T(1,128)} %bitcast.4, s32[1,2048]{1,0:T(1,128)} %bitcast.5), custom_call_target="tpu_custom_call" | custom-call | tf_op jit(solution)/shard_map/exchange/pallas_call | solution.py:336
  70.7 2.4 %relayout.1 = f32[64,8,1024]{2,1,0:T(8,128)} custom-call(f32[8,64,1024]{2,1,0:T(8,128)} %exchange.1.src), custom_call_target="tpu_custom_call" | custom-call | tf_op jit(solution)/shard_map/relayout/pallas_call | solution.py:346
